TPU v7x, 256 devices: a whole 4x4x8 slice. The times are simulated.
256 devices in a mesh: gx: 16 (over x, y_lo, core), gy: 16 (over y_hi, z).
Axes of the slice: x: 4, y: 4 (y_hi: 2, y_lo: 2; y = y_hi * 2 + y_lo), z: 8, core: 2. Of those that a mesh axis runs over, the one named last changes fastest.
Arguments:
- object_field: float32 [2, 1024, 1024], P(None, 'gy', 'gx'), may hold values from -1 to 1
- probe_modes: float32 [2, 1024, 128], P(None, ('gy', 'gx')), may hold values from -1.5 to 1.5
- positions: int32 [16, 16, 12, 2], P('gy', 'gx'), may hold values from 4 to 60, as said below
- amplitudes: float32 [16, 16, 12, 128, 128], P('gy', 'gx'), may hold values from 0 to 2
Outputs:
- object_out: float32 [2, 1024, 1024], P(None, 'gy', 'gx')
- probe_out: float32 [2, 1024, 128], P(None, ('gy', 'gx'))
Inputs may be any that keep to these rules, and one draw needn't show every extreme that they name: `positions`: each entry is a (row, column) inside its own tile; the centres of one tile lie at distinct cells of the 16 grid, each moved from the cell's middle by at most 4 cells along each dimension.
All inputs are finite; a program needn't handle non-finite values.
Results may differ from a plain program's by a relative error of at most 0.00065.
The roundings to bfloat16 on the way count: a program that leaves them out, or rounds other values in their place, can miss the bound.
Values sent between devices are 32-bit elements; how exact they have to be, the bound alone decides.
No kernel may reach another device: no remote copies, remote signals or barrier semaphores. Data moves between devices by JAX's collectives and lax.ppermute only.
A program may use at most 64 MiB of HBM per device.

v0:
```python
import math
import jax
import jax.numpy as jnp
from jax import lax
from jax.sharding import PartitionSpec as P

MODES = 8
ITERS = 2
SOFT_FLOOR = 0.05
OBJECT_REG = 1.0
PROBE_REG = 1.0


def from_behind(block, axis, distance):
    devices = range(lax.axis_size(axis))
    route = [(i - distance, i) for i in devices if i - distance in devices]
    return lax.ppermute(block, axis, route)


def extended_2(array, sides, width):
    for axis, dim in sides:
        peers, length = (lax.axis_size(axis), array.shape[dim])
        up = [(i, (i + 1) % peers) for i in range(peers - 1)]
        down = [(j, i) for i, j in up]
        last = lax.slice_in_dim(array, length - width, length, axis=dim)
        initial = lax.slice_in_dim(array, 0, width, axis=dim)
        before = lax.ppermute(last, axis, up)
        after = lax.ppermute(initial, axis, down)
        array = jnp.concatenate([before, array, after], axis=dim)
    return array


def tables(probe_side, sign_flip):
    indices = jnp.arange(probe_side, dtype=jnp.int32)
    phases = indices[:, None] * indices[None, :] % probe_side
    angles = phases.astype(jnp.float32) * (2.0 * math.pi / probe_side)
    factor = 1.0 / math.sqrt(probe_side)
    cosine = jnp.cos(angles) * factor
    sine_part = sign_flip * jnp.sin(angles) * factor
    left_op = jnp.stack(
        [jnp.stack([cosine, -sine_part]), jnp.stack([sine_part, cosine])]
    ).transpose(0, 2, 1, 3)
    right_op = jnp.stack(
        [jnp.stack([cosine, sine_part]), jnp.stack([-sine_part, cosine])]
    ).transpose(0, 2, 1, 3)
    return (left_op.astype(jnp.bfloat16), right_op.astype(jnp.bfloat16))


def transform(signal, operators):
    left_op, right_op = operators
    halfway = jnp.einsum(
        "dpcr,crmq->dpmq", left_op, signal, preferred_element_type=jnp.float32
    ).astype(jnp.bfloat16)
    return jnp.einsum("crmq,cqdk->drmk", halfway, right_op, preferred_element_type=jnp.float32)


def position_terms(patch_obj, probe, measured, forward, inverse):
    obj_real = patch_obj[0][:, None, :]
    obj_imag = patch_obj[1][:, None, :]
    wave_real = probe[0] * obj_real - probe[1] * obj_imag
    wave_imag = probe[0] * obj_imag + probe[1] * obj_real
    signal = jnp.stack([wave_real, wave_imag]).astype(jnp.bfloat16)
    spectrum = transform(signal, forward)
    intensity = jnp.sum(spectrum[0] * spectrum[0] + spectrum[1] * spectrum[1], axis=1)
    shrink = 1.0 - measured / jnp.sqrt(intensity + SOFT_FLOOR)
    residual = (spectrum * shrink[None, :, None, :]).astype(jnp.bfloat16)
    change = transform(residual, inverse)
    grad_real = jnp.sum(probe[0] * change[0] + probe[1] * change[1], axis=1)
    grad_imag = jnp.sum(probe[0] * change[1] - probe[1] * change[0], axis=1)
    probe_real = obj_real * change[0] + obj_imag * change[1]
    probe_imag = obj_real * change[1] - obj_imag * change[0]
    weight_probe = patch_obj[0] * patch_obj[0] + patch_obj[1] * patch_obj[1]
    return (jnp.stack([grad_real, grad_imag]), jnp.stack([probe_real, probe_imag]), weight_probe)


def fold_rows(gradient, margin, tile_side):
    extent = gradient.shape[1]
    for direction in (1, -1):
        rim_part = gradient[:, extent - margin :, :] if direction == 1 else gradient[:, :margin, :]
        offset = margin if direction == 1 else tile_side
        arrived = from_behind(rim_part, "gy", direction)
        gradient = gradient.at[:, offset : offset + margin, :].add(arrived)
    return gradient[:, margin : margin + tile_side, :]


def fold_cols(gradient, margin, tile_side):
    extent = gradient.shape[2]
    for direction in (1, -1):
        rim_part = gradient[:, :, extent - margin :] if direction == 1 else gradient[:, :, :margin]
        offset = margin if direction == 1 else tile_side
        arrived = from_behind(rim_part, "gx", direction)
        gradient = gradient.at[:, :, offset : offset + margin].add(arrived)
    return gradient[:, :, margin : margin + tile_side]


def unpack_probe(probe_rows, probe_side):
    return probe_rows.reshape(2, MODES, probe_side, probe_side).transpose(0, 2, 1, 3)


def local(object_field, probe_modes, positions, amplitudes):
    probe_side = amplitudes.shape[-1]
    margin = probe_side // 2
    tile_side = object_field.shape[1]
    centres = positions.reshape(-1, 2)
    measured_all = amplitudes.reshape(-1, probe_side, probe_side)
    forward = tables(probe_side, -1.0)
    inverse = tables(probe_side, 1.0)
    gathered = lax.all_gather(probe_modes, ("gy", "gx"), axis=1, tiled=True)
    probe = unpack_probe(gathered, probe_side)
    own_rows = probe_modes
    current = object_field
    for iteration in range(ITERS):
        extended = extended_2(current, (("gy", 1), ("gx", 2)), margin)
        weight_obj = jnp.sum(probe[0] * probe[0] + probe[1] * probe[1], axis=1)

        def visit(running, visit_item):
            grad_obj, grad_probe, weight_probe = running
            row_at, col_at, measured = visit_item
            zero_index = jnp.int32(0)
            patch_obj = lax.dynamic_slice(
                extended, (zero_index, row_at, col_at), (2, probe_side, probe_side)
            )
            g_obj, g_probe, w_probe = position_terms(patch_obj, probe, measured, forward, inverse)
            stacked = jnp.concatenate([g_obj, weight_obj[None]], axis=0)
            before = lax.dynamic_slice(
                grad_obj, (zero_index, row_at, col_at), (3, probe_side, probe_side)
            )
            grad_obj = lax.dynamic_update_slice(
                grad_obj, before + stacked, (zero_index, row_at, col_at)
            )
            return ((grad_obj, grad_probe + g_probe, weight_probe + w_probe), None)

        initial = (
            jnp.zeros((3, tile_side + probe_side, tile_side + probe_side), jnp.float32),
            jnp.zeros((2, probe_side, MODES, probe_side), jnp.float32),
            jnp.zeros((probe_side, probe_side), jnp.float32),
        )
        (grad_obj, grad_probe, weight_probe), _ = lax.scan(
            visit, initial, (centres[:, 0], centres[:, 1], measured_all)
        )
        folded = fold_cols(fold_rows(grad_obj, margin, tile_side), margin, tile_side)
        new_object = current - folded[0:2] / (folded[2] + OBJECT_REG)
        grad_rows = grad_probe.transpose(0, 2, 1, 3).reshape(2, MODES * probe_side, probe_side)
        totals, weight_total = lax.psum((grad_rows, weight_probe), ("gy", "gx"))
        whole_probe = probe.transpose(0, 2, 1, 3)
        whole_probe = whole_probe - totals.reshape(2, MODES, probe_side, probe_side) / (
            weight_total[None, None] + PROBE_REG
        )
        whole_probe = whole_probe.reshape(2, MODES * probe_side, probe_side)
        probe = unpack_probe(whole_probe, probe_side)
        row_count = own_rows.shape[1]
        own_rows = lax.dynamic_slice_in_dim(
            whole_probe, lax.axis_index(("gy", "gx")) * row_count, row_count, 1
        )
        current = new_object
    return (current, own_rows)


def solution(mesh):
    return jax.shard_map(
        local,
        mesh=mesh,
        in_specs=(
            P(None, "gy", "gx"),
            P(None, ("gy", "gx"), None),
            P("gy", "gx", None, None),
            P("gy", "gx", None, None, None),
        ),
        out_specs=(P(None, "gy", "gx"), P(None, ("gy", "gx"), None)),
        check_vma=False,
    )
```

profile of v0, /device:TPU:16, one launch (start us, length us, event | category | flops | bytes accessed | tf_op | source)
XLA Modules:
  0.0 1355.4 jit_solution(5158283582343708737)
XLA Ops:
  8.6 3.8 collective-permute-start
  12.4 5.6 collective-permute-start.1
  24.8 3.6 collective-permute-done.3
  29.3 362.2 %all-gather.2.cloned.1.call-done = f32[2,1024,128]{2,0,1:T(2,128)} async-done(((f32[2,4,128]{2,0,1:T(2,128)}), f32[2,1024,128]{2,0,1:T(2,128)}) %all-gather.2.cloned.1.call-update) | async-done | bytes 1048592 | tf_op jit(solution)/shard_map/all_gather | solution.py:108
  394.4 205.2 %while.38 = (s32[]{:T(128)}, f32[3,192,192]{2,1,0:T(8,128)}, f32[2,128,8,128]{3,1,0,2:T(8,128)}, f32[128,128]{1,0:T(8,128)}, s32[12]{0:T(128)S(1)}, /*index=5*/s...) while((s32[]{:T(128)}, f32[3,192,192]{2,1,0:T(8,128)}, ...), condition=%wide.region_5.6_spmd.clone, body=%wide.region_1.5_spmd.clone.sunk | while | flops 543391744 | bytes 27918840 | solution.py:138
  442.0 2.8 dynamic_update_slice.10
  493.3 2.8 dynamic_update_slice.10
  544.6 2.8 dynamic_update_slice.10
  578.8 2.9 dynamic_update_slice.10
  596.0 2.8 dynamic_update_slice.10
  603.5 6.7 collective-permute-start.5
  610.2 3.1 collective-permute-done.4
  623.0 7.7 collective-permute-start.9
  632.6 4.0 collective-permute-start.10
  637.9 3.2 collective-permute-done.11
  642.1 236.9 %all-reduce.7.cloned.1.call-done = (f32[2,1024,128]{2,0,1:T(2,128)}, f32[128,128]{1,0:T(8,128)}) async-done(((f32[2,1024,128]{2,0,1:T(2,128)}, f32[128,128]{1,0:T(8,128)}), (f32[2,1024,128]{2,0,1:T(2,128)}, f32[128,128]{1,0:T(8,128)})) %all-reduce.7.cloned.1.call-update) | async-done | bytes 1114128 | tf_op jit(solution)/shard_map/psum | solution.py:144
  882.9 197.0 %while.39 = (s32[]{:T(128)}, f32[3,192,192]{2,1,0:T(8,128)}, f32[2,128,8,128]{3,1,0,2:T(8,128)}, f32[128,128]{1,0:T(8,128)}, s32[12]{0:T(128)S(1)}, /*index=5*/s...) while((s32[]{:T(128)}, f32[3,192,192]{2,1,0:T(8,128)}, ...), condition=%wide.region_13.14_spmd.clone, body=%wide.region_9.13_spmd.clone.sunk | while | flops 543391744 | bytes 27918840 | solution.py:138
  928.4 2.8 dynamic_update_slice.11
  977.7 2.8 dynamic_update_slice.11
  1059.8 2.9 dynamic_update_slice.11
  1082.9 7.5 collective-permute-start.13
  1090.4 3.0 copy.30
  1097.3 3.0 collective-permute-done.15
  1101.9 244.8 %all-reduce.5.cloned.1.call-done = (f32[2,1024,128]{2,0,1:T(2,128)}, f32[128,128]{1,0:T(8,128)}) async-done(((f32[2,1024,128]{2,0,1:T(2,128)}, f32[128,128]{1,0:T(8,128)}), (f32[2,1024,128]{2,0,1:T(2,128)}, f32[128,128]{1,0:T(8,128)})) %all-reduce.5.cloned.1.call-update) | async-done | bytes 1114128 | tf_op jit(solution)/shard_map/psum | solution.py:144
  (713 shorter events, 335.3 us)
Async XLA Ops:
  7.2 384.3 %all-gather.2.cloned.1.call-start = ((), (), s32[]{:S(2)}) async-start(), calls=%async_computation | async-start | bytes 1052672 | tf_op jit(solution)/shard_map/all_gather | solution.py:108
  8.5 870.5 %all-reduce.7.cloned.1.call-start = ((), (), s32[]{:S(2)}) async-start(), calls=%async_computation.2 | async-start | bytes 2228224 | tf_op jit(solution)/shard_map/psum | solution.py:144
  8.6 11.9 collective-permute-start
  12.4 8.9 collective-permute-start.1
  21.4 3.5 collective-permute-start.2
  22.8 5.6 collective-permute-start.3
  577.9 3.7 copy-start.1
  599.6 18.5 %copy-start.2 = (f32[2,128,8,128]{3,1,0,2:T(8,128)S(1)}, f32[2,128,8,128]{3,1,0,2:T(8,128)}, u32[]{:S(2)}) copy-start(f32[2,128,8,128]{3,1,0,2:T(8,128)} %get-tuple-element.247) | copy-start | bytes 3145732
  600.7 12.5 collective-permute-start.4
  603.5 10.9 collective-permute-start.5
  615.5 4.5 collective-permute-start.6
  616.8 4.2 collective-permute-start.7
  619.9 260.0 %copy-start.13 = (f32[2,1024,128]{2,0,1:T(2,128)S(1)}, f32[2,1024,128]{2,0,1:T(2,128)}, u32[]{:S(2)}) copy-start(f32[2,1024,128]{2,0,1:T(2,128)} %all-gather.2.cloned.1.call-done) | copy-start | bytes 3145732
  619.9 726.8 %all-reduce.5.cloned.1.call-start = ((), (), s32[]{:S(2)}) async-start(), calls=%async_computation.1 | async-start | bytes 2228224 | tf_op jit(solution)/shard_map/psum | solution.py:144
  621.1 20.1 %copy-start.16 = (f32[2,64,64]{2,1,0:T(8,128)}, f32[2,64,64]{2,1,0:T(8,128)S(1)}, u32[]{:S(2)}) copy-start(f32[2,64,64]{2,1,0:T(8,128)S(1)} %fusion.68) | copy-start | bytes 98308
  621.1 9.9 collective-permute-start.8
  623.0 9.6 collective-permute-start.9
  632.6 5.3 collective-permute-start.10
  636.6 4.5 collective-permute-start.11
  1058.9 3.7 copy-start.4
  1081.0 12.5 collective-permute-start.12
  1082.9 10.7 collective-permute-start.13
  1094.6 2.7 collective-permute-start.14
  1095.9 4.4 collective-permute-start.15
  (172 other events, 219.7 us)
Sparse Core Ops, SparseCore 0:
  10.4 381.0 all-gather.1
  620.0 258.9 all-reduce.6
  1093.6 253.0 all-reduce.4
where the time goes:
time: 1360 us
  waiting for transfers between devices  861 us (63%)
  local copies, waits for them, and re-layouts  158 us (12%)
  other arithmetic  136 us (10%)
  loops' own time  88.1 us (6%)
  starting transfers between devices  51.3 us (4%)
  matrix products  46.9 us (3%)
  between operations  14.2 us (1%)
    psum x2, waiting for transfers between devices, local(): totals, weight_total = lax.psum((grad_rows, weight_probe), ('gy', 'gx'))  482 us
    all_gather x1, waiting for transfers between devices, local(): gathered = lax.all_gather(probe_modes, ('gy', 'gx'), axis=1, tiled=True)  362 us
    another operation x2, loops' own time, local(): lax.scan(visit, initial, (centres[:, 0], centres[:, 1], measured_all))  88.1 us
    dynamic_update_slice x24, local copies, waits for them, and re-layouts, visit(): lax.dynamic_update_slice(grad_obj, before + stacked, (zero_index, row_at,...  66.4 us
    add x48, other arithmetic, visit(): return ((grad_obj, grad_probe + g_probe, weight_probe + w_probe), None)  50.6 us
    while x336, local copies, waits for them, and re-layouts  49.5 us
    dot_general x48, matrix products, transform(): jnp.einsum('crmq,cqdk->drmk', halfway, right_op, preferred_element_type=j...  46.9 us
    sub x24, other arithmetic, position_terms(): shrink = 1.0 - measured / jnp.sqrt(intensity + SOFT_FLOOR)  35.8 us
  transfers between devices with their start and end apart: 19, of which 12 were waited for; matrix products, arithmetic and copies ran while one was open for 1% of the time, Pallas kernels for 0%

commit v1 on v0

--- a/solution.py
+++ b/solution.py
@@ -141,7 +141,7 @@
         folded = fold_cols(fold_rows(grad_obj, margin, tile_side), margin, tile_side)
         new_object = current - folded[0:2] / (folded[2] + OBJECT_REG)
         grad_rows = grad_probe.transpose(0, 2, 1, 3).reshape(2, MODES * probe_side, probe_side)
-        totals, weight_total = lax.psum((grad_rows, weight_probe), ("gy", "gx"))
+        totals, weight_total = lax.psum(lax.psum((grad_rows, weight_probe), "gx"), "gy")
         whole_probe = probe.transpose(0, 2, 1, 3)
         whole_probe = whole_probe - totals.reshape(2, MODES, probe_side, probe_side) / (
             weight_total[None, None] + PROBE_REG

time: 1360 us -> 1400 us (1.029)
  waiting for transfers between devices: 861 us -> 891 us
    psum x2 -> x4, waiting for transfers between devices: 482 us -> 512 us  [the longest x2 291 us: local(): lax.psum(lax.psum((grad_rows, weight_probe), 'gx'), 'gy')]
  transfers between devices with their start and end apart: 19 -> 21, of which waited for: 12 -> 13; matrix products, arithmetic and copies ran while one was open for 1% -> 0% of each run, Pallas kernels for 0% -> 0%
where the time goes in v1:
time: 1400 us
  waiting for transfers between devices  891 us (64%)
  local copies, waits for them, and re-layouts  162 us (12%)
  other arithmetic  134 us (10%)
  loops' own time  97.6 us (7%)
  starting transfers between devices  50.6 us (4%)
  matrix products  46.9 us (3%)
  between operations  14.3 us (1%)
    all_gather x1, waiting for transfers between devices, local(): gathered = lax.all_gather(probe_modes, ('gy', 'gx'), axis=1, tiled=True)  362 us
    psum x2, waiting for transfers between devices, local(): lax.psum(lax.psum((grad_rows, weight_probe), 'gx'), 'gy')  291 us
    psum x2, waiting for transfers between devices, local(): lax.psum((grad_rows, weight_probe), 'gx')  221 us
    another operation x2, loops' own time, local(): lax.scan(visit, initial, (centres[:, 0], centres[:, 1], measured_all))  97.6 us
    dynamic_update_slice x24, local copies, waits for them, and re-layouts, visit(): lax.dynamic_update_slice(grad_obj, before + stacked, (zero_index, row_at,...  66.4 us
    add x48, other arithmetic, visit(): return ((grad_obj, grad_probe + g_probe, weight_probe + w_probe), None)  50.8 us
    while x336, local copies, waits for them, and re-layouts  49.8 us
    dot_general x48, matrix products, transform(): jnp.einsum('crmq,cqdk->drmk', halfway, right_op, preferred_element_type=j...  46.9 us
  transfers between devices with their start and end apart: 21, of which 13 were waited for; matrix products, arithmetic and copies ran while one was open for 0% of the time, Pallas kernels for 0%

profile of v1, /device:TPU:16, one launch (start us, length us, event | category | flops | bytes accessed | tf_op | source)
XLA Modules:
  0.0 1396.6 jit_solution(8334570063082131564)
XLA Ops:
  8.6 3.8 collective-permute-start
  12.4 5.6 collective-permute-start.1
  24.8 3.6 collective-permute-done.3
  29.3 362.2 %all-gather.2.cloned.1.call-done = f32[2,1024,128]{2,0,1:T(2,128)} async-done(((f32[2,4,128]{2,0,1:T(2,128)}), f32[2,1024,128]{2,0,1:T(2,128)}) %all-gather.2.cloned.1.call-update) | async-done | bytes 1048592 | tf_op jit(solution)/shard_map/all_gather | solution.py:108
  394.4 205.6 %while.38 = (s32[]{:T(128)}, f32[3,192,192]{2,1,0:T(8,128)}, f32[2,128,8,128]{3,1,0,2:T(8,128)}, f32[128,128]{1,0:T(8,128)}, s32[12]{0:T(128)S(1)}, /*index=5*/s...) while((s32[]{:T(128)}, f32[3,192,192]{2,1,0:T(8,128)}, ...), condition=%wide.region_5.6_spmd.clone, body=%wide.region_1.5_spmd.clone.sunk | while | flops 543391744 | bytes 27918840 | solution.py:138
  442.1 2.8 dynamic_update_slice.10
  493.5 2.8 dynamic_update_slice.10
  579.1 2.9 dynamic_update_slice.10
  600.0 3.0 copy.24
  606.9 6.7 collective-permute-start.5
  613.6 3.6 collective-permute-done.4
  618.4 107.5 %all-reduce.15.cloned.1.call-done = (f32[2,1024,128]{2,0,1:T(2,128)}, f32[128,128]{1,0:T(8,128)}) async-done(((f32[2,1024,128]{2,0,1:T(2,128)}, f32[128,128]{1,0:T(8,128)}), (f32[2,1024,128]{2,0,1:T(2,128)}, f32[128,128]{1,0:T(8,128)})) %all-reduce.15.cloned.1.call-update) | async-done | bytes 1114128 | tf_op jit(solution)/shard_map/psum | solution.py:144
  730.8 3.5 collective-permute-start.8
  734.3 6.0 collective-permute-start.9
  742.2 3.2 collective-permute-start.10
  750.2 136.7 %all-reduce.11.cloned.1.call-done = (f32[2,1024,128]{2,0,1:T(2,128)}, f32[128,128]{1,0:T(8,128)}) async-done(((f32[2,1024,128]{2,0,1:T(2,128)}, f32[128,128]{1,0:T(8,128)}), (f32[2,1024,128]{2,0,1:T(2,128)}, f32[128,128]{1,0:T(8,128)})) %all-reduce.11.cloned.1.call-update) | async-done | bytes 1114128 | tf_op jit(solution)/shard_map/psum | solution.py:144
  890.8 209.3 %while.39 = (s32[]{:T(128)}, f32[3,192,192]{2,1,0:T(8,128)}, f32[2,128,8,128]{3,1,0,2:T(8,128)}, f32[128,128]{1,0:T(8,128)}, s32[12]{0:T(128)S(1)}, /*index=5*/s...) while((s32[]{:T(128)}, f32[3,192,192]{2,1,0:T(8,128)}, ...), condition=%wide.region_15.16_spmd.clone, body=%wide.region_11.15_spmd.clone.sunk | while | flops 543391744 | bytes 27918840 | solution.py:138
  939.4 2.8 dynamic_update_slice.11
  991.7 2.8 dynamic_update_slice.11
  1078.9 2.9 dynamic_update_slice.11
  1100.0 3.0 copy.30
  1106.5 7.1 collective-permute-start.13
  1113.6 113.9 %all-reduce.13.cloned.1.call-done = (f32[2,1024,128]{2,0,1:T(2,128)}, f32[128,128]{1,0:T(8,128)}) async-done(((f32[2,1024,128]{2,0,1:T(2,128)}, f32[128,128]{1,0:T(8,128)}), (f32[2,1024,128]{2,0,1:T(2,128)}, f32[128,128]{1,0:T(8,128)})) %all-reduce.13.cloned.1.call-update) | async-done | bytes 1114128 | tf_op jit(solution)/shard_map/psum | solution.py:144
  1233.8 154.1 %all-reduce.9.cloned.1.call-done = (f32[2,1024,128]{2,0,1:T(2,128)}, f32[128,128]{1,0:T(8,128)}) async-done(((f32[2,1024,128]{2,0,1:T(2,128)}, f32[128,128]{1,0:T(8,128)}), (f32[2,1024,128]{2,0,1:T(2,128)}, f32[128,128]{1,0:T(8,128)})) %all-reduce.9.cloned.1.call-update) | async-done | bytes 1114128 | tf_op jit(solution)/shard_map/psum | solution.py:144
  (721 shorter events, 344.1 us)
Async XLA Ops:
  7.2 384.3 %all-gather.2.cloned.1.call-start = ((), (), s32[]{:S(2)}) async-start(), calls=%async_computation | async-start | bytes 1052672 | tf_op jit(solution)/shard_map/all_gather | solution.py:108
  8.5 717.4 %all-reduce.15.cloned.1.call-start = ((), (), s32[]{:S(2)}) async-start(), calls=%async_computation.4 | async-start | bytes 2228224 | tf_op jit(solution)/shard_map/psum | solution.py:144
  8.6 11.9 collective-permute-start
  12.4 8.9 collective-permute-start.1
  21.4 3.5 collective-permute-start.2
  22.8 5.6 collective-permute-start.3
  603.1 283.8 %all-reduce.11.cloned.1.call-start = ((), (), s32[]{:S(2)}) async-start(), calls=%async_computation.2 | async-start | bytes 2228224 | tf_op jit(solution)/shard_map/psum | solution.py:144
  604.1 13.1 collective-permute-start.4
  606.9 11.4 collective-permute-start.5
  725.9 501.7 %all-reduce.13.cloned.1.call-start = ((), (), s32[]{:S(2)}) async-start(), calls=%async_computation.3 | async-start | bytes 2228224 | tf_op jit(solution)/shard_map/psum | solution.py:144
  726.0 4.8 copy-start.22
  726.0 2.7 collective-permute-start.6
  727.3 160.5 %copy-start.14 = (f32[2,1024,128]{2,0,1:T(2,128)S(1)}, f32[2,1024,128]{2,0,1:T(2,128)}, u32[]{:S(2)}) copy-start(f32[2,1024,128]{2,0,1:T(2,128)} %all-gather.2.cloned.1.call-done) | copy-start | bytes 3145732
  727.3 3.3 collective-permute-start.7
  730.8 18.5 %copy-start.17 = (f32[2,64,64]{2,1,0:T(8,128)}, f32[2,64,64]{2,1,0:T(8,128)S(1)}, u32[]{:S(2)}) copy-start(f32[2,64,64]{2,1,0:T(8,128)S(1)} %fusion.68) | copy-start | bytes 98308
  730.8 9.8 collective-permute-start.8
  734.3 7.9 collective-permute-start.9
  742.2 4.5 collective-permute-start.10
  745.4 3.9 collective-permute-start.11
  1103.1 284.8 %all-reduce.9.cloned.1.call-start = ((), (), s32[]{:S(2)}) async-start(), calls=%async_computation.1 | async-start | bytes 2228224 | tf_op jit(solution)/shard_map/psum | solution.py:144
  1104.2 123.4 %collective-permute-start.12 = (f32[3,64,192]{2,1,0:T(8,128)S(1)}, f32[3,64,192]{2,1,0:T(8,128)S(1)}, u32[]{:S(2)}, u32[]{:S(2)}) collective-permute-start(f32[3,64,192]{2,1,0:T(8,128)S(1)} %get-tuple-element.486), channel_id=1, source_target_pairs={{0,1},{1,2},{2,3},{3,4},{4,5},{5,6},{6,7},{7,8},{8,9},{9,10},{10,1... | collective-permute-start | bytes 442376 | tf_op jit(solution)/shard_map/ppermute | solution.py:17
  1106.5 121.1 %collective-permute-start.13 = (f32[3,64,192]{2,1,0:T(8,128)S(1)}, f32[3,64,192]{2,1,0:T(8,128)S(1)}, u32[]{:S(2)}, u32[]{:S(2)}) collective-permute-start(f32[3,64,192]{2,1,0:T(8,128)S(1)} %get-tuple-element.487), channel_id=1, source_target_pairs={{1,0},{2,1},{3,2},{4,3},{5,4},{6,5},{7,6},{8,7},{9,8},{10,9},{11,1... | collective-permute-start | bytes 442376 | tf_op jit(solution)/shard_map/ppermute | solution.py:17
  1227.7 2.7 collective-permute-start.14
  1229.0 3.2 collective-permute-start.15
  (175 other events, 228.5 us)
Sparse Core Ops, SparseCore 0:
  10.4 381.0 all-gather.1
  603.2 122.6 all-reduce.14
  728.6 158.2 all-reduce.10
  1103.2 124.3 all-reduce.12
  1230.2 157.6 all-reduce.8
